TPU v7x, 32 devices: a whole 2x2x4 slice. The times are simulated.
32 devices in a mesh: ia: 4 (over z), ja: 2 (over y), ka: 4 (over x, core).
Axes of the slice: x: 2, y: 2, z: 4, core: 2. Of those that a mesh axis runs over, the one named last changes fastest.
Arguments:
- tile_values: bfloat16 [768, 128], P(('ia', 'ja', 'ka')), may hold values from -0.59765625 to 0.59765625
- tile_rows: int32 [768, 128], P(('ia', 'ja', 'ka')), may hold values from 0 to 63
- tile_cols: int32 [768, 128], P(('ia', 'ja', 'ka')), may hold values from 0 to 2047
- tile_depths: int32 [768, 128], P(('ia', 'ja', 'ka')), may hold values from 0 to 1023
- tile_live: int32 [32, 8], P(('ia', 'ja', 'ka')), may hold values from 0 to 3, as said below
- factor_b: bfloat16 [16, 2, 2048], P(None, 'ja', ('ia', 'ka')), may hold values from -6 to 6
- factor_c: bfloat16 [16, 4, 1024], P(None, 'ka', ('ia', 'ja')), may hold values from -6 to 6
- proj: float32 [16, 256], replicated, may hold values from -0.375 to 0.375
Outputs:
- tucker_y: float32 [2048, 256], P(('ia', 'ja', 'ka'))
- gram: float32 [256, 256], replicated
- new_factor: float32 [16, 2048], P(None, ('ia', 'ja', 'ka'))
Inputs may be any that keep to these rules, and one draw needn't show every extreme that they name: tile_live[d, o] counts the live leading slots among the 3 slots that device d holds for the device at index o along ja+ka within its mode-1 block; in every draw there is an owner for which every device has all 3 slots live, and every device has some owner with all 3 slots live.
All inputs are finite; a program needn't handle non-finite values.
Results may differ from a plain program's by a relative error of at most 0.0041.
Values may be sent and summed in bfloat16 or wider, within the bound.
A program may use at most 64 MiB of HBM per device.

v0:
```python
import jax
import jax.numpy as jnp
from jax import lax
from jax.sharding import PartitionSpec as P

RANK = 16
ROWS_DEV = 64


def owner_block(scaled, depth_rows, target):
    kron_rows = (scaled[:, None] * depth_rows[None, :]).reshape(
        scaled.shape[0] * depth_rows.shape[0], -1
    )
    onehot = (target.reshape(1, -1) == lax.iota(jnp.int32, ROWS_DEV)[:, None]).astype(jnp.bfloat16)
    return lax.dot_general(
        onehot, kron_rows, (((1,), (1,)), ((), ())), preferred_element_type=jnp.float32
    )


def group_blocks(scaled, depth_rows, target, begin_slot, pair_size, slot_count):
    rank_size = scaled.shape[0]
    tile_width = scaled.shape[2]
    scaled_part = lax.dynamic_slice_in_dim(scaled, begin_slot, pair_size * slot_count, 1)
    depth_part = lax.dynamic_slice_in_dim(depth_rows, begin_slot, pair_size * slot_count, 1)
    target_part = lax.dynamic_slice_in_dim(target, begin_slot, pair_size * slot_count, 0)
    scaled_part = scaled_part.reshape(rank_size, pair_size, slot_count, tile_width)
    depth_part = depth_part.reshape(depth_rows.shape[0], pair_size, slot_count, tile_width)
    target_part = target_part.reshape(pair_size, slot_count, tile_width)
    return jax.vmap(owner_block, in_axes=(1, 1, 0))(scaled_part, depth_part, target_part)


def owner_total(scaled, depth_rows, target, groups, slot_count):
    pair_size = 2
    columns = scaled.shape[0] * depth_rows.shape[0]
    result = jnp.zeros((ROWS_DEV, columns), jnp.float32)

    def turn(turn_index, result):
        begin_slot = turn_index * pair_size * slot_count
        blocks = group_blocks(scaled, depth_rows, target, begin_slot, pair_size, slot_count)
        return result + jnp.sum(blocks, axis=0)

    return lax.fori_loop(0, groups // pair_size, turn, result)


def on_device(tile_values, tile_rows, tile_cols, tile_depths, tile_live, factor_b, factor_c, proj):
    owners = lax.axis_size("ja") * lax.axis_size("ka")
    slot_total = tile_values.shape[0]
    slot_count = slot_total // owners
    mode_two = lax.all_gather(factor_b, ("ia", "ka"), axis=2, tiled=True)[:, 0, :]
    mode_three = lax.all_gather(factor_c, ("ia", "ja"), axis=2, tiled=True)[:, 0, :]
    slot_index = lax.iota(jnp.int32, slot_total)
    owner_of = slot_index // slot_count
    counts = jnp.sum(
        jnp.where(owner_of[:, None] == lax.iota(jnp.int32, owners)[None, :], tile_live, 0), axis=1
    )
    is_live = slot_index % slot_count < counts
    target = jnp.where(is_live[:, None], tile_rows, ROWS_DEV)
    scaled = (
        tile_values.astype(jnp.float32)[None]
        * jnp.take(mode_two, tile_cols, axis=1).astype(jnp.float32)
    ).astype(jnp.bfloat16)
    depth_rows = jnp.take(mode_three, tile_depths, axis=1)
    payload = jnp.concatenate([scaled, depth_rows], axis=0)
    arrived, routed = (
        lax.all_to_all(payload, ("ja", "ka"), split_axis=1, concat_axis=1, tiled=True),
        lax.all_to_all(target[None], ("ja", "ka"), split_axis=1, concat_axis=1, tiled=True),
    )
    summed = owner_total(arrived[:RANK], arrived[RANK:], routed[0], owners, slot_count)
    local_gram = lax.dot_general(
        summed,
        summed,
        (((0,), (0,)), ((), ())),
        precision=lax.Precision.HIGHEST,
        preferred_element_type=jnp.float32,
    )
    gram_total = lax.psum(local_gram, ("ia", "ja", "ka"))
    gram = gram_total / (ROWS_DEV * owners * lax.axis_size("ia"))
    new_factor = lax.dot_general(
        proj,
        summed,
        (((1,), (1,)), ((), ())),
        precision=lax.Precision.HIGHEST,
        preferred_element_type=jnp.float32,
    )
    return (summed, gram, new_factor)


def solution(mesh):
    return jax.shard_map(
        on_device,
        mesh=mesh,
        in_specs=(
            P(("ia", "ja", "ka"), None),
            P(("ia", "ja", "ka"), None),
            P(("ia", "ja", "ka"), None),
            P(("ia", "ja", "ka"), None),
            P(("ia", "ja", "ka"), None),
            P(None, "ja", ("ia", "ka")),
            P(None, "ka", ("ia", "ja")),
            P(),
        ),
        out_specs=(P(("ia", "ja", "ka"), None), P(), P(None, ("ia", "ja", "ka"))),
        check_vma=False,
    )
```

profile of v0, /device:TPU:0, one launch (start us, length us, event | category | flops | bytes accessed | tf_op | source)
XLA Modules:
  0.0 239.9 jit_solution(6678735856828618585)
XLA Ops:
  7.2 0.0 copy-start
  7.2 0.0 copy-start.2
  7.2 0.8 bitcast_clamp_fusion.1
  8.0 0.0 copy-done.2
  8.0 0.0 copy-start.3
  8.0 0.7 copy-done.3
  8.7 0.0 copy-start.6
  8.7 0.7 copy-done.6
  9.4 0.1 copy.29
  9.5 24.6 %all_gather.6 = bf16[16,1,2048]{0,2,1:T(8,128)(2,1)S(1)} all-gather(bf16[16,1,128]{0,2,1:T(8,128)(2,1)S(1)} %copy.29), channel_id=1, replica_groups=mesh['ia'=4,'ja'=2,'ka'=4] {'ia','ka'}, dimensions={2}, use_global_device_ids=true | all-gather | bytes 69632 | tf_op jit(solution)/shard_map/all_gather | solution.py:49
  34.1 9.2 %gather_fusion = bf16[3072,16]{1,0:T(8,128)(2,1)S(1)} fusion(bf16[16,2048]{0,1:T(8,128)(2,1)S(1)} %bitcast.41, s32[3072]{0:T(1024)S(1)} %bitcast_clamp_fusion.1), kind=kCustom, calls=%fused_computation | custom fusion | bytes 208896 | tf_op jit(solution)/shard_map/jit(_take)/gather | solution.py:60
  43.3 0.0 copy-start.5
  43.3 0.3 copy.30
  43.5 0.4 copy-done.5
  44.0 0.0 copy-start.7
  44.0 0.7 copy-done.7
  44.6 0.1 copy.31
  44.8 30.8 %all_gather.7 = bf16[16,1,1024]{0,2,1:T(8,128)(2,1)S(1)} all-gather(bf16[16,1,128]{0,2,1:T(8,128)(2,1)S(1)} %copy.31), channel_id=1, replica_groups=mesh['ia'=4,'ja'=2,'ka'=4] {'ia','ja'}, dimensions={2}, use_global_device_ids=true | all-gather | bytes 36864 | tf_op jit(solution)/shard_map/all_gather | solution.py:50
  75.5 9.2 %gather_fusion.1 = bf16[3072,16]{1,0:T(8,128)(2,1)S(1)} fusion(bf16[16,1024]{0,1:T(8,128)(2,1)S(1)} %bitcast.40, s32[3072]{0:T(1024)S(1)} %bitcast_clamp_fusion), kind=kCustom, calls=%fused_computation.1 | custom fusion | bytes 208896 | tf_op jit(solution)/shard_map/jit(_take)/gather | solution.py:62
  84.7 0.3 copy.32
  85.0 0.7 pad_maximum_fusion
  85.7 0.0 copy-start.4
  85.7 3.5 %all-to-all-start.1 = ((bf16[32,24,128]{2,0,1:T(8,128)(2,1)}), bf16[32,24,128]{2,0,1:T(8,128)(2,1)S(1)}, u32[]{:S(2)}, u32[]{:S(2)}) async-start(bf16[32,24,128]{2,0,1:T(8,128)(2,1)} %pad_maximum_fusion), calls=%async_computation.1 | async-start | bytes 393216 | tf_op jit(solution)/shard_map/all_to_all | solution.py:65
  89.3 0.0 copy-start.8
  89.3 0.6 copy-done.8
  90.0 0.1 select_reduce_fusion
  90.1 0.0 copy-done.4
  90.1 0.7 broadcast_select_fusion
  90.7 4.7 %all-to-all-done.1 = bf16[32,24,128]{2,0,1:T(8,128)(2,1)S(1)} async-done(((bf16[32,24,128]{2,0,1:T(8,128)(2,1)}), bf16[32,24,128]{2,0,1:T(8,128)(2,1)S(1)}, u32[]{:S(2)}, u32[]{:S(2)}) %all-to-all-start.1) | async-done | bytes 196640 | tf_op jit(solution)/shard_map/all_to_all | solution.py:65
  95.4 3.3 %all-to-all-start = ((s32[1,24,128]{2,0,1:T(1,128)}), s32[1,24,128]{2,0,1:T(1,128)S(1)}, u32[]{:S(2)}, u32[]{:S(2)}) async-start(s32[1,24,128]{2,0,1:T(1,128)} %bitcast.1), calls=%async_computation | async-start | bytes 24576 | tf_op jit(solution)/shard_map/all_to_all | solution.py:66
  98.7 0.0 all-reduce.2.cloned.1.call-start
  98.8 4.6 %all-to-all-done = s32[1,24,128]{2,0,1:T(1,128)S(1)} async-done(((s32[1,24,128]{2,0,1:T(1,128)}), s32[1,24,128]{2,0,1:T(1,128)S(1)}, u32[]{:S(2)}, u32[]{:S(2)}) %all-to-all-start) | async-done | bytes 12320 | tf_op jit(solution)/shard_map/all_to_all | solution.py:66
  103.4 3.7 %while.16 = (s32[]{:T(128)}, f32[64,256]{1,0:T(8,128)S(1)}, s32[24,128]{1,0:T(8,128)S(1)}, bf16[16,24,128]{2,0,1:T(8,128)(2,1)S(1)}, bf16[16,24,128]{2,0,1:T(8,1...) while((s32[]{:T(128)}, f32[64,256]{1,0:T(8,128)S(1)}, s32[24,128]{1,0:T(8,128)S(1)}, ...), condition=%wide.region_2.3_spmd.clone, body=%wide.region_1.2_spmd.clone.sunk | while | flops 25444360 | bytes 1965213 | solution.py:42
  103.5 0.2 broadcast_multiply_fusion.3
  103.7 0.3 mul.80
  104.0 0.3 fusion.14
  104.4 0.2 broadcast_multiply_fusion.3
  104.6 0.3 mul.80
  105.0 0.3 fusion.14
  105.3 0.2 broadcast_multiply_fusion.3
  105.5 0.3 mul.80
  105.9 0.3 fusion.14
  106.3 0.2 broadcast_multiply_fusion.3
  106.5 0.3 mul.80
  106.9 0.3 fusion.14
  107.1 0.0 copy-start.1
  107.2 1.1 fusion.5
  108.3 0.0 all-reduce.2.cloned.1.call-update
  108.3 0.0 copy-done.1
  108.3 0.0 copy-done
  108.3 0.8 convolution_bitcast_fusion.1
  109.1 122.3 %all-reduce.2.cloned.1.call-done = f32[256,256]{1,0:T(8,128)} async-done(((f32[256,256]{1,0:T(8,128)}), f32[256,256]{1,0:T(8,128)}) %all-reduce.2.cloned.1.call-update) | async-done | bytes 262160 | tf_op jit(solution)/shard_map/psum | solution.py:76
  231.4 1.7 broadcast_multiply_fusion.1
  (30 shorter events, 0.4 us)
Async XLA Ops:
  7.2 101.2 %copy-start = (f32[16,256]{1,0:T(8,128)S(1)}, f32[16,256]{1,0:T(8,128)}, u32[]{:S(2)}) copy-start(f32[16,256]{1,0:T(8,128)} %param.17) | copy-start | bytes 49156
  7.2 0.8 copy-start.2
  8.0 0.7 copy-start.3
  8.7 0.7 copy-start.6
  43.3 0.7 copy-start.5
  44.0 0.7 copy-start.7
  85.7 4.3 %copy-start.4 = (s32[24,128]{1,0:T(8,128)S(1)}, s32[24,128]{1,0:T(8,128)}, u32[]{:S(2)}) copy-start(s32[24,128]{1,0:T(8,128)} %param.11) | copy-start | bytes 36868
  85.7 9.7 %all-to-all-start.1 = ((bf16[32,24,128]{2,0,1:T(8,128)(2,1)}), bf16[32,24,128]{2,0,1:T(8,128)(2,1)S(1)}, u32[]{:S(2)}, u32[]{:S(2)}) async-start(bf16[32,24,128]{2,0,1:T(8,128)(2,1)} %pad_maximum_fusion), calls=%async_computation.1 | async-start | bytes 393216 | tf_op jit(solution)/shard_map/all_to_all | solution.py:65
  89.3 0.7 copy-start.8
  95.4 8.0 %all-to-all-start = ((s32[1,24,128]{2,0,1:T(1,128)}), s32[1,24,128]{2,0,1:T(1,128)S(1)}, u32[]{:S(2)}, u32[]{:S(2)}) async-start(s32[1,24,128]{2,0,1:T(1,128)} %bitcast.1), calls=%async_computation | async-start | bytes 24576 | tf_op jit(solution)/shard_map/all_to_all | solution.py:66
  98.7 132.6 %all-reduce.2.cloned.1.call-start = ((), (), s32[]{:S(2)}) async-start(), calls=%async_computation.2 | async-start | bytes 524288 | tf_op jit(solution)/shard_map/psum | solution.py:76
  107.1 1.2 copy-start.1
Sparse Core Ops, SparseCore 0:
  108.4 122.8 all-reduce.1
where the time goes:
time: 240 us
  waiting for transfers between devices  132 us (55%)
  blocking collectives  55.4 us (23%)
  local copies, waits for them, and re-layouts  23.8 us (10%)
  between operations  14.2 us (6%)
  starting transfers between devices  6.9 us (3%)
  other arithmetic  4.78 us (2%)
  matrix products  2.99 us (1%)
    psum x1, waiting for transfers between devices, on_device(): gram_total = lax.psum(local_gram, ('ia', 'ja', 'ka'))  122 us
    all_gather x1, blocking collectives, on_device(): lax.all_gather(factor_c, ('ia', 'ja'), axis=2, tiled=True)[:, 0, :]  30.8 us
    all_gather x1, blocking collectives, on_device(): lax.all_gather(factor_b, ('ia', 'ka'), axis=2, tiled=True)[:, 0, :]  24.6 us
    gather x2, local copies, waits for them, and re-layouts, on_device(): depth_rows = jnp.take(mode_three, tile_depths, axis=1)  9.41 us
    gather x2, local copies, waits for them, and re-layouts, on_device(): jnp.take(mode_two, tile_cols, axis=1).astype(jnp.float32)  9.41 us
  transfers between devices with their start and end apart: 3, of which 3 were waited for; matrix products, arithmetic and copies ran while one was open for 1% of the time, Pallas kernels for 0%

commit v1 on v0

--- a/solution.py
+++ b/solution.py
@@ -73,7 +73,8 @@
         precision=lax.Precision.HIGHEST,
         preferred_element_type=jnp.float32,
     )
-    gram_total = lax.psum(local_gram, ("ia", "ja", "ka"))
+    inner = lax.psum(local_gram, ("ja", "ka"))
+    gram_total = lax.psum(inner, "ia")
     gram = gram_total / (ROWS_DEV * owners * lax.axis_size("ia"))
     new_factor = lax.dot_general(
         proj,

time: 240 us -> 205 us (0.85)
  waiting for transfers between devices: 132 us -> 96.2 us
    psum x1 -> x2, waiting for transfers between devices: 122 us -> 86.9 us  [the longest x1 50.3 us: on_device(): inner = lax.psum(local_gram, ('ja', 'ka'))]
  transfers between devices with their start and end apart: 3 -> 4, of which waited for: 3 -> 4; matrix products, arithmetic and copies ran while one was open for 1% -> 1% of each run, Pallas kernels for 0% -> 0%
where the time goes in v1:
time: 205 us
  waiting for transfers between devices  96.2 us (47%)
  blocking collectives  55.4 us (27%)
  local copies, waits for them, and re-layouts  23.8 us (12%)
  between operations  14.2 us (7%)
  starting transfers between devices  6.94 us (3%)
  other arithmetic  4.78 us (2%)
  matrix products  2.99 us (1%)
    psum x1, waiting for transfers between devices, on_device(): inner = lax.psum(local_gram, ('ja', 'ka'))  50.3 us
    psum x1, waiting for transfers between devices, on_device(): gram_total = lax.psum(inner, 'ia')  36.5 us
    all_gather x1, blocking collectives, on_device(): lax.all_gather(factor_c, ('ia', 'ja'), axis=2, tiled=True)[:, 0, :]  30.8 us
    all_gather x1, blocking collectives, on_device(): lax.all_gather(factor_b, ('ia', 'ka'), axis=2, tiled=True)[:, 0, :]  24.6 us
    gather x2, local copies, waits for them, and re-layouts, on_device(): depth_rows = jnp.take(mode_three, tile_depths, axis=1)  9.41 us
    gather x2, local copies, waits for them, and re-layouts, on_device(): jnp.take(mode_two, tile_cols, axis=1).astype(jnp.float32)  9.41 us
    all_to_all x1, waiting for transfers between devices, on_device(): lax.all_to_all(payload, ('ja', 'ka'), split_axis=1, concat_axis=1, tiled=...  4.68 us
    all_to_all x1, waiting for transfers between devices, on_device(): lax.all_to_all(target[None], ('ja', 'ka'), split_axis=1, concat_axis=1, t...  4.59 us
  transfers between devices with their start and end apart: 4, of which 4 were waited for; matrix products, arithmetic and copies ran while one was open for 1% of the time, Pallas kernels for 0%

profile of v1, /device:TPU:0, one launch (start us, length us, event | category | flops | bytes accessed | tf_op | source)
XLA Modules:
  0.0 204.5 jit_solution(6119360781119444534)
XLA Ops:
  7.2 0.0 copy-start
  7.2 0.0 copy-start.2
  7.2 0.8 bitcast_clamp_fusion.1
  8.0 0.0 copy-done.2
  8.0 0.0 copy-start.3
  8.0 0.7 copy-done.3
  8.7 0.0 copy-start.6
  8.7 0.7 copy-done.6
  9.4 0.1 copy.29
  9.5 24.6 %all_gather.6 = bf16[16,1,2048]{0,2,1:T(8,128)(2,1)S(1)} all-gather(bf16[16,1,128]{0,2,1:T(8,128)(2,1)S(1)} %copy.29), channel_id=1, replica_groups=mesh['ia'=4,'ja'=2,'ka'=4] {'ia','ka'}, dimensions={2}, use_global_device_ids=true | all-gather | bytes 69632 | tf_op jit(solution)/shard_map/all_gather | solution.py:49
  34.1 9.2 %gather_fusion = bf16[3072,16]{1,0:T(8,128)(2,1)S(1)} fusion(bf16[16,2048]{0,1:T(8,128)(2,1)S(1)} %bitcast.41, s32[3072]{0:T(1024)S(1)} %bitcast_clamp_fusion.1), kind=kCustom, calls=%fused_computation | custom fusion | bytes 208896 | tf_op jit(solution)/shard_map/jit(_take)/gather | solution.py:60
  43.3 0.0 copy-start.5
  43.3 0.3 copy.30
  43.5 0.4 copy-done.5
  44.0 0.0 copy-start.7
  44.0 0.7 copy-done.7
  44.6 0.1 copy.31
  44.8 30.8 %all_gather.7 = bf16[16,1,1024]{0,2,1:T(8,128)(2,1)S(1)} all-gather(bf16[16,1,128]{0,2,1:T(8,128)(2,1)S(1)} %copy.31), channel_id=1, replica_groups=mesh['ia'=4,'ja'=2,'ka'=4] {'ia','ja'}, dimensions={2}, use_global_device_ids=true | all-gather | bytes 36864 | tf_op jit(solution)/shard_map/all_gather | solution.py:50
  75.5 9.2 %gather_fusion.1 = bf16[3072,16]{1,0:T(8,128)(2,1)S(1)} fusion(bf16[16,1024]{0,1:T(8,128)(2,1)S(1)} %bitcast.40, s32[3072]{0:T(1024)S(1)} %bitcast_clamp_fusion), kind=kCustom, calls=%fused_computation.1 | custom fusion | bytes 208896 | tf_op jit(solution)/shard_map/jit(_take)/gather | solution.py:62
  84.7 0.3 copy.32
  85.0 0.7 pad_maximum_fusion
  85.7 0.0 copy-start.4
  85.7 3.5 %all-to-all-start.1 = ((bf16[32,24,128]{2,0,1:T(8,128)(2,1)}), bf16[32,24,128]{2,0,1:T(8,128)(2,1)S(1)}, u32[]{:S(2)}, u32[]{:S(2)}) async-start(bf16[32,24,128]{2,0,1:T(8,128)(2,1)} %pad_maximum_fusion), calls=%async_computation.1 | async-start | bytes 393216 | tf_op jit(solution)/shard_map/all_to_all | solution.py:65
  89.3 0.0 copy-start.8
  89.3 0.6 copy-done.8
  90.0 0.1 select_reduce_fusion
  90.1 0.0 copy-done.4
  90.1 0.7 broadcast_select_fusion
  90.7 4.7 %all-to-all-done.1 = bf16[32,24,128]{2,0,1:T(8,128)(2,1)S(1)} async-done(((bf16[32,24,128]{2,0,1:T(8,128)(2,1)}), bf16[32,24,128]{2,0,1:T(8,128)(2,1)S(1)}, u32[]{:S(2)}, u32[]{:S(2)}) %all-to-all-start.1) | async-done | bytes 196640 | tf_op jit(solution)/shard_map/all_to_all | solution.py:65
  95.4 3.3 %all-to-all-start = ((s32[1,24,128]{2,0,1:T(1,128)}), s32[1,24,128]{2,0,1:T(1,128)S(1)}, u32[]{:S(2)}, u32[]{:S(2)}) async-start(s32[1,24,128]{2,0,1:T(1,128)} %bitcast.1), calls=%async_computation | async-start | bytes 24576 | tf_op jit(solution)/shard_map/all_to_all | solution.py:66
  98.7 0.0 all-reduce.3.cloned.1.call-start
  98.8 4.6 %all-to-all-done = s32[1,24,128]{2,0,1:T(1,128)S(1)} async-done(((s32[1,24,128]{2,0,1:T(1,128)}), s32[1,24,128]{2,0,1:T(1,128)S(1)}, u32[]{:S(2)}, u32[]{:S(2)}) %all-to-all-start) | async-done | bytes 12320 | tf_op jit(solution)/shard_map/all_to_all | solution.py:66
  103.4 3.7 %while.16 = (s32[]{:T(128)}, f32[64,256]{1,0:T(8,128)S(1)}, s32[24,128]{1,0:T(8,128)S(1)}, bf16[16,24,128]{2,0,1:T(8,128)(2,1)S(1)}, bf16[16,24,128]{2,0,1:T(8,1...) while((s32[]{:T(128)}, f32[64,256]{1,0:T(8,128)S(1)}, s32[24,128]{1,0:T(8,128)S(1)}, ...), condition=%wide.region_2.3_spmd.clone, body=%wide.region_1.2_spmd.clone.sunk | while | flops 25444360 | bytes 1965213 | solution.py:42
  103.5 0.2 broadcast_multiply_fusion.3
  103.7 0.3 mul.80
  104.0 0.3 fusion.14
  104.4 0.2 broadcast_multiply_fusion.3
  104.6 0.3 mul.80
  105.0 0.3 fusion.14
  105.3 0.2 broadcast_multiply_fusion.3
  105.5 0.3 mul.80
  105.9 0.3 fusion.14
  106.3 0.2 broadcast_multiply_fusion.3
  106.5 0.3 mul.80
  106.9 0.3 fusion.14
  107.1 0.0 copy-start.1
  107.2 1.1 fusion.5
  108.3 0.0 all-reduce.3.cloned.1.call-update
  108.3 0.0 all-reduce.5.cloned.1.call-start
  108.4 50.3 %all-reduce.3.cloned.1.call-done = f32[256,256]{1,0:T(8,128)} async-done(((f32[256,256]{1,0:T(8,128)}), f32[256,256]{1,0:T(8,128)}) %all-reduce.3.cloned.1.call-update) | async-done | bytes 262160 | tf_op jit(solution)/shard_map/psum | solution.py:76
  158.7 0.0 all-reduce.5.cloned.1.call-update
  158.7 0.0 copy-done.1
  158.7 0.0 copy-done
  158.7 0.8 convolution_bitcast_fusion.1
  159.5 36.5 %all-reduce.5.cloned.1.call-done = f32[256,256]{1,0:T(8,128)} async-done(((f32[256,256]{1,0:T(8,128)}), f32[256,256]{1,0:T(8,128)}) %all-reduce.5.cloned.1.call-update) | async-done | bytes 262160 | tf_op jit(solution)/shard_map/psum | solution.py:77
  196.0 1.7 broadcast_multiply_fusion.1
  (30 shorter events, 0.4 us)
Async XLA Ops:
  7.2 151.6 %copy-start = (f32[16,256]{1,0:T(8,128)S(1)}, f32[16,256]{1,0:T(8,128)}, u32[]{:S(2)}) copy-start(f32[16,256]{1,0:T(8,128)} %param.17) | copy-start | bytes 49156
  7.2 0.8 copy-start.2
  8.0 0.7 copy-start.3
  8.7 0.7 copy-start.6
  43.3 0.7 copy-start.5
  44.0 0.7 copy-start.7
  85.7 4.3 %copy-start.4 = (s32[24,128]{1,0:T(8,128)S(1)}, s32[24,128]{1,0:T(8,128)}, u32[]{:S(2)}) copy-start(s32[24,128]{1,0:T(8,128)} %param.11) | copy-start | bytes 36868
  85.7 9.7 %all-to-all-start.1 = ((bf16[32,24,128]{2,0,1:T(8,128)(2,1)}), bf16[32,24,128]{2,0,1:T(8,128)(2,1)S(1)}, u32[]{:S(2)}, u32[]{:S(2)}) async-start(bf16[32,24,128]{2,0,1:T(8,128)(2,1)} %pad_maximum_fusion), calls=%async_computation.1 | async-start | bytes 393216 | tf_op jit(solution)/shard_map/all_to_all | solution.py:65
  89.3 0.7 copy-start.8
  95.4 8.0 %all-to-all-start = ((s32[1,24,128]{2,0,1:T(1,128)}), s32[1,24,128]{2,0,1:T(1,128)S(1)}, u32[]{:S(2)}, u32[]{:S(2)}) async-start(s32[1,24,128]{2,0,1:T(1,128)} %bitcast.1), calls=%async_computation | async-start | bytes 24576 | tf_op jit(solution)/shard_map/all_to_all | solution.py:66
  98.7 59.9 %all-reduce.3.cloned.1.call-start = ((), (), s32[]{:S(2)}) async-start(), calls=%async_computation.2 | async-start | bytes 524288 | tf_op jit(solution)/shard_map/psum | solution.py:76
  107.1 51.6 %copy-start.1 = (f32[64,256]{1,0:T(8,128)}, f32[64,256]{1,0:T(8,128)S(1)}, u32[]{:S(2)}) copy-start(f32[64,256]{1,0:T(8,128)S(1)} %get-tuple-element.132) | copy-start | bytes 196612
  108.3 87.7 %all-reduce.5.cloned.1.call-start = ((), (), s32[]{:S(2)}) async-start(), calls=%async_computation.3 | async-start | bytes 524288 | tf_op jit(solution)/shard_map/psum | solution.py:77
Sparse Core Ops, SparseCore 0:
  108.4 50.2 all-reduce.2
  161.0 34.9 all-reduce.4
